TPU v7x, 128 devices: a whole 4x4x4 slice. The times are simulated.
128 devices in a mesh: group: 8 (over y, core), member: 16 (over z, x).
Axes of the slice: x: 4, y: 4, z: 4, core: 2. Of those that a mesh axis runs over, the one named last changes fastest.
Arguments:
- hidden: bfloat16 [49152, 3584], P(('group', 'member')), may hold values from -30 to 30
- projection: bfloat16 [3584, 1024], replicated, may hold values from -0.09375 to 0.09375
- inv_temp: float32 [1], replicated, may hold values from 10 to 80
- partners: int32 [128, 12], P(('group', 'member')), may hold values from 0 to 127, as said below
- positives: int32 [49152], P(('group', 'member')), may hold values from 0 to 49151, as said below
Outputs:
- loss: float32 [], replicated
- grad_hidden: bfloat16 [49152, 3584], P(('group', 'member'))
- grad_proj: float32 [3584, 1024], P(('group', 'member'))
Inputs may be any that keep to these rules, and one draw needn't show every extreme that they name: Block ids are numbered in row order. partners[b] are 12 distinct blocks of b's own group of 16 consecutive blocks, none equal to b; within a group they are b's index in the group XORed with 12 distinct nonzero offsets common to that group, so b lists c exactly when c lists b. positives pairs the rows of each block among themselves: positives_i lies in i's block, differs from i, and positives of positives_i is i.
All inputs are finite; a program needn't handle non-finite values.
Results may differ from a plain program's by a relative error of at most 0.006.
Values may be sent and summed in bfloat16 or wider, within the bound.
No kernel may reach another device: no remote copies, remote signals or barrier semaphores. Data moves between devices by JAX's collectives and lax.ppermute only.
A program may use at most 128 MiB of HBM per device.

v0:
```python
import jax
import jax.numpy as jnp
from jax import lax
from jax.sharding import PartitionSpec as P

epsilon = 1e-06


def per_device(hidden, projection, inv_temp, partners, positives):
    rows = hidden.shape[0]
    width = projection.shape[1]
    members = lax.axis_size("member")
    groups = lax.axis_size("group")
    mine = lax.axis_index("member")
    projected = jnp.dot(hidden, projection, preferred_element_type=jnp.float32)
    lengths = jnp.sqrt(jnp.sum(projected * projected, axis=1, keepdims=True) + epsilon)
    unit_rows = projected / lengths
    unit_low = unit_rows.astype(jnp.bfloat16)
    gathered = lax.all_gather(unit_low, "member", axis=0, tiled=True).reshape(members, rows, width)
    chosen = jnp.concatenate([mine[None], partners[0] % members])
    others = gathered[chosen]
    scale = inv_temp[0]
    tiles_count = partners.shape[1] + 1
    first = (jnp.arange(tiles_count) == 0)[:, None, None]
    columns = jnp.arange(rows)
    self_mask = first & (columns[:, None] == columns[None, :])[None]
    scores = scale * jnp.einsum("id,pjd->pij", unit_low, others, preferred_element_type=jnp.float32)
    scores = jnp.where(self_mask, -jnp.inf, scores)
    highest = jnp.max(scores, axis=(0, 2))
    log_totals = highest + jnp.log(jnp.sum(jnp.exp(scores - highest[None, :, None]), axis=(0, 2)))
    local_pos = positives % rows
    target = first & (columns[None, None, :] == local_pos[:, None][None])
    pos_scores = jnp.sum(jnp.where(target, scores, 0.0), axis=(0, 2))
    total = lax.psum(jnp.sum(log_totals - pos_scores), ("group", "member"))
    loss = total / (groups * members * rows)
    all_totals = lax.all_gather(log_totals, "member", axis=0, tiled=True).reshape(members, rows)
    row_prob = jnp.exp(scores - log_totals[None, :, None])
    col_prob = jnp.exp(scores - all_totals[chosen][:, None, :])
    weights = (row_prob + col_prob - 2.0 * target).astype(jnp.bfloat16)
    grad_unit = scale * jnp.einsum(
        "pij,pjd->id", weights, others, preferred_element_type=jnp.float32
    )
    along = jnp.sum(unit_rows * grad_unit, axis=1, keepdims=True)
    grad_projected = ((grad_unit - unit_rows * along) / lengths).astype(jnp.bfloat16)
    grad_hidden = lax.dot_general(
        grad_projected, projection, (((1,), (1,)), ((), ())), preferred_element_type=jnp.float32
    ).astype(jnp.bfloat16)
    grad_proj = lax.psum_scatter(
        lax.dot_general(
            hidden, grad_projected, (((0,), (0,)), ((), ())), preferred_element_type=jnp.float32
        ),
        ("group", "member"),
        scatter_dimension=0,
        tiled=True,
    )
    return (loss, grad_hidden, grad_proj)


def solution(mesh):
    return jax.shard_map(
        per_device,
        mesh=mesh,
        in_specs=(
            P(("group", "member"), None),
            P(),
            P(),
            P(("group", "member"), None),
            P(("group", "member")),
        ),
        out_specs=(P(), P(("group", "member"), None), P(("group", "member"), None)),
        check_vma=False,
    )
```

profile of v0, /device:TPU:1, one launch (start us, length us, event | category | flops | bytes accessed | tf_op | source)
XLA Modules:
  0.0 362.2 jit_solution(9420817212567875197)
XLA Ops:
  7.2 0.0 copy-start
  7.2 0.0 all-gather.3.cloned.1.call-start
  7.2 1.7 copy-done
  8.9 5.4 %multiply_reduce_fusion.1 = (f32[384]{0:T(512)S(1)}, f32[384,1024]{1,0:T(8,128)S(1)}) fusion(bf16[384,3584]{1,0:T(8,128)(2,1)S(1)} %copy-done, bf16[3584,1024]{1,0:T(8,128)(2,1)} %param.6), kind=kOutput, calls=%fused_computation.22 | convolution fusion | flops 2819358208 | bytes 11666944 | tf_op jit(solution)/shard_map/dot_general | solution.py:15
  14.4 1.2 copy-done.2
  15.5 1.1 fusion.22
  16.6 0.0 all-gather.3.cloned.1.call-update
  16.7 0.0 all-reduce.3.cloned.1.call-start
  17.4 0.1 fusion.18
  17.5 0.7 iota_compare_fusion.1
  18.2 0.7 iota_compare_fusion
  19.0 91.2 %all-gather.3.cloned.1.call-done = bf16[6144,1024]{1,0:T(8,128)(2,1)} async-done(((bf16[384,1024]{1,0:T(8,128)(2,1)}), bf16[6144,1024]{1,0:T(8,128)(2,1)}) %all-gather.3.cloned.1.call-update) | async-done | bytes 12582928 | tf_op jit(solution)/shard_map/all_gather | solution.py:19
  110.2 10.4 %gather_fusion = bf16[13,384,1024]{2,1,0:T(8,128)(2,1)} fusion(bf16[16,384,1024]{2,1,0:T(8,128)(2,1)} %bitcast.47, s32[1024]{0:T(1024)S(1)} %pad_clamp_fusion), kind=kCustom, calls=%fused_computation | custom fusion | bytes 20447284 | tf_op jit(solution)/shard_map/gather | solution.py:21
  120.5 10.0 %fusion.11 = (f32[384]{0:T(512)S(1)}, f32[13,384,384]{2,1,0:T(8,128)S(1)}) fusion(f32[]{:T(128)} %bitcast.44, pred[384,384]{0,1:T(8,128)(4,1)} %iota_compare_fusion.1, pred[13]{0:T(512)(128)(4,1)S(1)} %iota_compare_fusion.2, bf16[13,384,1024]{2,1,0:T(8,128)(2,1)} %gather_fusion, bf16[384,1024]{1,0:T(8,128)(2,1)S(1)} %copy-done.4), kind=kOutput, calls=%fused_computation.18 | convolution fusion | flops 3933535744 | bytes 18826768 | tf_op jit(solution)/shard_map/id,pjd->pij/dot_general | solution.py:27
  130.5 0.0 copy-start.1
  130.5 0.0 copy-done.6
  130.5 0.0 copy-done.8
  130.5 0.0 copy-start.7
  130.5 0.0 copy-start.9
  130.6 3.2 fusion
  133.8 0.6 subtract_reduce_fusion
  134.4 17.7 %all-gather = f32[16,1,384]{2,1,0:T(1,128)S(1)} all-gather(f32[1,1,384]{2,1,0:T(1,128)S(1)} %reshape.161), channel_id=1, replica_groups=mesh['group'=8,'member'=16] {'member'}, dimensions={0}, use_global_device_ids=true | all-gather | bytes 26112 | tf_op jit(solution)/shard_map/all_gather | solution.py:36
  152.1 0.6 gather_fusion.1
  152.7 12.8 %multiply_reduce_fusion = (f32[384]{0:T(512)S(1)}, f32[384,1024]{1,0:T(8,128)S(1)}) fusion(f32[384,1024]{1,0:T(8,128)} %copy-done.2, f32[384]{0:T(512)S(1)} %add_sqrt_fusion, bf16[13,384,1024]{2,1,0:T(8,128)(2,1)} %gather_fusion, f32[13,384]{1,0:T(8,128)S(1)} %gather_fusion.1, f32[384]{0:T(512)S(1)} %get-tuple-element.12, ...), kind=kOutput, calls=%fused_computation.21 | convolution fusion | flops 3946610176 | bytes 21356560 | tf_op jit(solution)/shard_map/pij,pjd->id/dot_general | solution.py:40
  165.5 1.1 copy-done.5
  166.6 7.5 %convolution_bitcast_fusion = f32[3584,1024]{0,1:T(8,128)} fusion(bf16[384,3584]{1,0:T(8,128)(2,1)S(1)} %copy-done, f32[384,1024]{1,0:T(8,128)S(1)} %get-tuple-element.18, f32[384]{0:T(512)S(1)} %get-tuple-element.17, f32[384]{0:T(512)S(1)} %add_sqrt_fusion, f32[384,1024]{1,0:T(8,128)S(1)} %copy-done.3), kind=kOutput, calls=%fused_computation.4 | convolution fusion | flops 2820538368 | bytes 20581376 | tf_op jit(solution)/shard_map/dot_general | solution.py:49
  174.2 0.0 all-reduce.3.cloned.1.call-update
  174.2 69.1 %psum.7 = f32[]{:T(128)} all-reduce(f32[]{:T(128)} %get-tuple-element.11), channel_id=1, replica_groups=mesh['group'=8,'member'=16] {'group','member'}, use_global_device_ids=true, to_apply=%region_5.6 | all-reduce | flops 1 | bytes 8 | tf_op jit(solution)/shard_map/psum | solution.py:34
  243.9 8.8 %convolution_convert_fusion = bf16[384,3584]{1,0:T(8,128)(2,1)} fusion(bf16[3584,1024]{1,0:T(8,128)(2,1)} %param.6, f32[384,1024]{1,0:T(8,128)} %copy-done.5, f32[384]{0:T(512)S(1)} %get-tuple-element.17, f32[384]{0:T(512)S(1)} %add_sqrt_fusion, f32[384,1024]{1,0:T(8,128)} %copy-done.2), kind=kOutput, calls=%fused_computation.10 | convolution fusion | flops 2821914624 | bytes 13241344 | tf_op jit(solution)/shard_map/dot_general | solution.py:45
  252.7 99.2 %all-reduce.3.cloned.1.call-done = f32[3584,1024]{0,1:T(8,128)} async-done(((f32[3584,1024]{0,1:T(8,128)}), f32[3584,1024]{0,1:T(8,128)}) %all-reduce.3.cloned.1.call-update) | async-done | bytes 14680080
  352.0 1.4 constant_dynamic-slice_fusion
  353.4 0.9 copy.11
  (22 shorter events, 0.1 us)
Async XLA Ops:
  7.2 1.8 copy-start
  7.2 10.2 %copy-start.11 = (s32[1,12]{1,0:T(1,128)S(1)}, s32[1,12]{1,0:T(1,128)}, u32[]{:S(2)}) copy-start(s32[1,12]{1,0:T(1,128)} %param.8) | copy-start | bytes 148
  7.2 11.0 %copy-start.10 = (s32[384]{0:T(512)S(1)}, s32[384]{0:T(512)}, u32[]{:S(2)}) copy-start(s32[384]{0:T(512)} %param.9) | copy-start | bytes 4612
  7.2 103.0 %all-gather.3.cloned.1.call-start = ((), (), s32[]{:S(2)}) async-start(), calls=%async_computation | async-start | bytes 13369344 | tf_op jit(solution)/shard_map/all_gather | solution.py:19
  14.3 1.2 copy-start.2
  16.7 335.3 %all-reduce.3.cloned.1.call-start = ((), (), s32[]{:S(2)}) async-start(), calls=%async_computation.1 | async-start | bytes 29360128
  110.2 10.4 %copy-start.4 = (bf16[384,1024]{1,0:T(8,128)(2,1)S(1)}, bf16[384,1024]{1,0:T(8,128)(2,1)}, u32[]{:S(2)}) copy-start(bf16[384,1024]{1,0:T(8,128)(2,1)} %fusion.22) | copy-start | bytes 2359300
  120.5 10.0 %copy-start.6 = (pred[384,384]{0,1:T(8,128)(4,1)S(1)}, pred[384,384]{0,1:T(8,128)(4,1)}, u32[]{:S(2)}) copy-start(pred[384,384]{0,1:T(8,128)(4,1)} %iota_compare_fusion.1) | copy-start | bytes 442372
  120.5 10.0 %copy-start.8 = (pred[384,384]{0,1:T(8,128)(4,1)S(1)}, pred[384,384]{0,1:T(8,128)(4,1)}, u32[]{:S(2)}) copy-start(pred[384,384]{0,1:T(8,128)(4,1)} %iota_compare_fusion) | copy-start | bytes 442372
  130.5 3.2 copy-start.1
  130.5 22.1 %copy-start.7 = (pred[384,384]{0,1:T(8,128)(4,1)S(1)}, pred[384,384]{0,1:T(8,128)(4,1)}, u32[]{:S(2)}) copy-start(pred[384,384]{0,1:T(8,128)(4,1)} %iota_compare_fusion.1) | copy-start | bytes 442372
  130.5 22.1 %copy-start.9 = (pred[384,384]{0,1:T(8,128)(4,1)S(1)}, pred[384,384]{0,1:T(8,128)(4,1)}, u32[]{:S(2)}) copy-start(pred[384,384]{0,1:T(8,128)(4,1)} %iota_compare_fusion) | copy-start | bytes 442372
  152.7 13.9 %copy-start.3 = (f32[384,1024]{1,0:T(8,128)S(1)}, f32[384,1024]{1,0:T(8,128)}, u32[]{:S(2)}) copy-start(f32[384,1024]{1,0:T(8,128)} %copy-done.2) | copy-start | bytes 4718596
  165.5 1.1 copy-start.5
Sparse Core Ops, SparseCore 0:
  16.8 93.3 all-gather.2
  174.3 177.6 all-reduce.2
where the time goes:
time: 362 us
  waiting for transfers between devices  190 us (52%)
  blocking collectives  86.8 us (24%)
  matrix products  44.5 us (12%)
  local copies, waits for them, and re-layouts  17.3 us (5%)
  between operations  16.6 us (5%)
  other arithmetic  6.46 us (2%)
    unnamed x3, waiting for transfers between devices  99.2 us
    all_gather x1, waiting for transfers between devices, per_device(): lax.all_gather(unit_low, 'member', axis=0, tiled=True)  91.2 us
    psum x1, blocking collectives, per_device(): total = lax.psum(jnp.sum(log_totals - pos_scores), ('group', 'member'))  69.1 us
    all_gather x1, blocking collectives, per_device(): lax.all_gather(log_totals, 'member', axis=0, tiled=True)  17.7 us
    dot_general x1, matrix products, per_device(): jnp.einsum('pij,pjd->id', weights, others, preferred_element_type=jnp.flo...  12.8 us
    gather x1, local copies, waits for them, and re-layouts, per_device(): others = gathered[chosen]  10.4 us
    dot_general x1, matrix products, per_device(): jnp.einsum('id,pjd->pij', unit_low, others, preferred_element_type=jnp.fl...  9.95 us
    dot_general x1, matrix products, per_device(): lax.dot_general(grad_projected, projection, (((1,), (1,)), ((), ())), pre...  8.83 us
  transfers between devices with their start and end apart: 2, of which 2 were waited for; matrix products, arithmetic and copies ran while one was open for 3% of the time, Pallas kernels for 0%

commit v1 on v0

--- a/solution.py
+++ b/solution.py
@@ -16,7 +16,9 @@
     lengths = jnp.sqrt(jnp.sum(projected * projected, axis=1, keepdims=True) + epsilon)
     unit_rows = projected / lengths
     unit_low = unit_rows.astype(jnp.bfloat16)
-    gathered = lax.all_gather(unit_low, "member", axis=0, tiled=True).reshape(members, rows, width)
+    gathered = jnp.concatenate(
+        lax.all_to_all(jnp.stack([unit_low] * lax.axis_size("member")), "member", 0, 0), axis=0
+    ).reshape(members, rows, width)
     chosen = jnp.concatenate([mine[None], partners[0] % members])
     others = gathered[chosen]
     scale = inv_temp[0]

time: 362 us -> 472 us (1.30)
  waiting for transfers between devices: 190 us -> 282 us
  local copies, waits for them, and re-layouts: 17.3 us -> 26.4 us
  starting transfers between devices: 0.08 us -> 8.65 us
    all_to_all x0 -> x1, waiting for transfers between devices: none -> 184 us  [per_device(): lax.all_to_all(jnp.stack([unit_low] * lax.axis_size('member')), 'member',...]
    all_gather x1 -> x0, waiting for transfers between devices: 91.2 us -> none  [per_device(): lax.all_gather(unit_low, 'member', axis=0, tiled=True)]
    all_to_all x0 -> x1, starting transfers between devices: none -> 8.6 us  [per_device(): lax.all_to_all(jnp.stack([unit_low] * lax.axis_size('member')), 'member',...]
    another operation x0 -> x1, local copies, waits for them, and re-layouts: none -> 6.09 us  [per_device(): jnp.stack([unit_low] * lax.axis_size('member'))]
    unnamed x3 -> x2, waiting for transfers between devices: 99.2 us -> 98.5 us
  transfers between devices with their start and end apart: 2 -> 2, of which waited for: 2 -> 2; matrix products, arithmetic and copies ran while one was open for 3% -> 2% of each run, Pallas kernels for 0% -> 0%
where the time goes in v1:
time: 472 us; the launch traced here: 471 us
  waiting for transfers between devices  282 us (60%)
  blocking collectives  87.7 us (19%)
  matrix products  44.4 us (9%)
  local copies, waits for them, and re-layouts  26.4 us (6%)
  between operations  16.6 us (4%)
  starting transfers between devices  8.65 us (2%)
  other arithmetic  5.58 us (1%)
    all_to_all x1, waiting for transfers between devices, per_device(): lax.all_to_all(jnp.stack([unit_low] * lax.axis_size('member')), 'member',...  184 us
    unnamed x2, waiting for transfers between devices  98.5 us
    psum x1, blocking collectives, per_device(): total = lax.psum(jnp.sum(log_totals - pos_scores), ('group', 'member'))  71.4 us
    all_gather x1, blocking collectives, per_device(): lax.all_gather(log_totals, 'member', axis=0, tiled=True)  16.3 us
    dot_general x1, matrix products, per_device(): jnp.einsum('pij,pjd->id', weights, others, preferred_element_type=jnp.flo...  12.8 us
    gather x1, local copies, waits for them, and re-layouts, per_device(): others = gathered[chosen]  10.3 us
    dot_general x1, matrix products, per_device(): jnp.einsum('id,pjd->pij', unit_low, others, preferred_element_type=jnp.fl...  9.91 us
  transfers between devices with their start and end apart: 2, of which 2 were waited for; matrix products, arithmetic and copies ran while one was open for 2% of the time, Pallas kernels for 0%

profile of v1, /device:TPU:1, one launch (start us, length us, event | category | flops | bytes accessed | tf_op | source)
XLA Modules:
  0.0 471.4 jit_solution(17229548271596959876)
XLA Ops:
  7.2 0.0 copy-start
  7.2 1.8 copy-done
  8.9 5.4 %multiply_reduce_fusion.1 = (f32[384]{0:T(512)S(1)}, f32[384,1024]{1,0:T(8,128)S(1)}) fusion(bf16[384,3584]{1,0:T(8,128)(2,1)S(1)} %copy-done, bf16[3584,1024]{1,0:T(8,128)(2,1)} %param.6), kind=kOutput, calls=%fused_computation.22 | convolution fusion | flops 2819358208 | bytes 11666944 | tf_op jit(solution)/shard_map/dot_general | solution.py:15
  14.4 1.2 copy-done.2
  15.5 0.2 fusion.22
  15.8 6.1 %stack.2 = bf16[16,384,1024]{2,1,0:T(8,128)(2,1)} broadcast(bf16[384,1024]{1,0:T(8,128)(2,1)S(1)} %fusion.22), dimensions={1,2} | broadcast | bytes 13369344 | tf_op jit(solution)/shard_map/stack | solution.py:20
  21.9 8.6 %all-to-all-start = ((bf16[16,384,1024]{2,1,0:T(8,128)(2,1)}), bf16[16,384,1024]{2,1,0:T(8,128)(2,1)}, u32[]{:S(2)}, u32[]{:S(2)}) async-start(bf16[16,384,1024]{2,1,0:T(8,128)(2,1)} %stack.2), calls=%async_computation | async-start | bytes 25165824 | tf_op jit(solution)/shard_map/all_to_all | solution.py:20
  30.5 0.0 all-reduce.3.cloned.1.call-start
  31.2 0.0 copy-done.10
  31.2 0.1 fusion.18
  31.3 0.7 iota_compare_fusion.1
  32.0 0.0 copy-done.9
  32.0 0.8 iota_compare_fusion
  32.8 183.7 %all-to-all-done = bf16[16,384,1024]{2,1,0:T(8,128)(2,1)} async-done(((bf16[16,384,1024]{2,1,0:T(8,128)(2,1)}), bf16[16,384,1024]{2,1,0:T(8,128)(2,1)}, u32[]{:S(2)}, u32[]{:S(2)}) %all-to-all-start) | async-done | bytes 12582944 | tf_op jit(solution)/shard_map/all_to_all | solution.py:20
  216.4 10.3 %gather_fusion = bf16[13,384,1024]{2,1,0:T(8,128)(2,1)} fusion(bf16[16,384,1024]{2,1,0:T(8,128)(2,1)} %all-to-all-done, s32[1024]{0:T(1024)S(1)} %pad_clamp_fusion), kind=kCustom, calls=%fused_computation | custom fusion | bytes 20447284 | tf_op jit(solution)/shard_map/gather | solution.py:23
  226.7 9.9 %fusion.11 = (f32[384]{0:T(512)S(1)}, f32[13,384,384]{2,1,0:T(8,128)S(1)}) fusion(f32[]{:T(128)} %bitcast.43, pred[384,384]{0,1:T(8,128)(4,1)} %iota_compare_fusion.1, pred[13]{0:T(512)(128)(4,1)S(1)} %iota_compare_fusion.2, bf16[13,384,1024]{2,1,0:T(8,128)(2,1)} %gather_fusion, bf16[384,1024]{1,0:T(8,128)(2,1)S(1)} %fusion.22), kind=kOutput, calls=%fused_computation.18 | convolution fusion | flops 3933535744 | bytes 18826768 | tf_op jit(solution)/shard_map/id,pjd->pij/dot_general | solution.py:29
  236.7 0.0 copy-start.8
  236.7 3.0 copy-done.1
  239.7 0.0 copy-done.5
  239.7 3.2 fusion
  242.9 0.6 subtract_reduce_fusion
  243.5 16.3 %all-gather = f32[16,1,384]{2,1,0:T(1,128)S(1)} all-gather(f32[1,1,384]{2,1,0:T(1,128)S(1)} %reshape.159), channel_id=1, replica_groups=mesh['group'=8,'member'=16] {'member'}, dimensions={0}, use_global_device_ids=true | all-gather | bytes 26112 | tf_op jit(solution)/shard_map/all_gather | solution.py:38
  259.8 0.6 gather_fusion.1
  260.4 12.8 %multiply_reduce_fusion = (f32[384]{0:T(512)S(1)}, f32[384,1024]{1,0:T(8,128)S(1)}) fusion(f32[384,1024]{1,0:T(8,128)} %copy-done.2, f32[384]{0:T(512)S(1)} %add_sqrt_fusion, bf16[13,384,1024]{2,1,0:T(8,128)(2,1)} %gather_fusion, f32[13,384]{1,0:T(8,128)S(1)} %gather_fusion.1, f32[384]{0:T(512)S(1)} %get-tuple-element.12, ...), kind=kOutput, calls=%fused_computation.21 | convolution fusion | flops 3946610176 | bytes 21356560 | tf_op jit(solution)/shard_map/pij,pjd->id/dot_general | solution.py:42
  273.1 1.1 copy-done.4
  274.3 7.5 %convolution_bitcast_fusion = f32[3584,1024]{0,1:T(8,128)} fusion(bf16[384,3584]{1,0:T(8,128)(2,1)S(1)} %copy-done, f32[384,1024]{1,0:T(8,128)S(1)} %get-tuple-element.18, f32[384]{0:T(512)S(1)} %get-tuple-element.17, f32[384]{0:T(512)S(1)} %add_sqrt_fusion, f32[384,1024]{1,0:T(8,128)S(1)} %copy-done.3), kind=kOutput, calls=%fused_computation.4 | convolution fusion | flops 2820538368 | bytes 20581376 | tf_op jit(solution)/shard_map/dot_general | solution.py:51
  281.8 0.0 all-reduce.3.cloned.1.call-update
  281.9 71.4 %psum.7 = f32[]{:T(128)} all-reduce(f32[]{:T(128)} %get-tuple-element.11), channel_id=1, replica_groups=mesh['group'=8,'member'=16] {'group','member'}, use_global_device_ids=true, to_apply=%region_5.6 | all-reduce | flops 1 | bytes 8 | tf_op jit(solution)/shard_map/psum | solution.py:36
  353.9 8.8 %convolution_convert_fusion = bf16[384,3584]{1,0:T(8,128)(2,1)} fusion(bf16[3584,1024]{1,0:T(8,128)(2,1)} %param.6, f32[384,1024]{1,0:T(8,128)} %copy-done.4, f32[384]{0:T(512)S(1)} %get-tuple-element.17, f32[384]{0:T(512)S(1)} %add_sqrt_fusion, f32[384,1024]{1,0:T(8,128)} %copy-done.2), kind=kOutput, calls=%fused_computation.10 | convolution fusion | flops 2821914624 | bytes 13241344 | tf_op jit(solution)/shard_map/dot_general | solution.py:47
  362.7 98.4 %all-reduce.3.cloned.1.call-done = f32[3584,1024]{0,1:T(8,128)} async-done(((f32[3584,1024]{0,1:T(8,128)}), f32[3584,1024]{0,1:T(8,128)}) %all-reduce.3.cloned.1.call-update) | async-done | bytes 14680080
  461.2 1.4 constant_dynamic-slice_fusion
  462.6 0.9 copy.11
  (20 shorter events, 0.1 us)
Async XLA Ops:
  7.2 1.8 copy-start
  14.3 1.2 copy-start.2
  21.9 9.3 %copy-start.10 = (s32[1,12]{1,0:T(1,128)S(1)}, s32[1,12]{1,0:T(1,128)}, u32[]{:S(2)}) copy-start(s32[1,12]{1,0:T(1,128)} %param.8) | copy-start | bytes 148
  21.9 10.2 %copy-start.9 = (s32[384]{0:T(512)S(1)}, s32[384]{0:T(512)}, u32[]{:S(2)}) copy-start(s32[384]{0:T(512)} %param.9) | copy-start | bytes 4612
  21.9 194.6 %all-to-all-start = ((bf16[16,384,1024]{2,1,0:T(8,128)(2,1)}), bf16[16,384,1024]{2,1,0:T(8,128)(2,1)}, u32[]{:S(2)}, u32[]{:S(2)}) async-start(bf16[16,384,1024]{2,1,0:T(8,128)(2,1)} %stack.2), calls=%async_computation | async-start | bytes 25165824 | tf_op jit(solution)/shard_map/all_to_all | solution.py:20
  30.5 430.7 %all-reduce.3.cloned.1.call-start = ((), (), s32[]{:S(2)}) async-start(), calls=%async_computation.1 | async-start | bytes 29360128
  226.7 13.0 %copy-start.5 = (pred[384,384]{0,1:T(8,128)(4,1)S(1)}, pred[384,384]{0,1:T(8,128)(4,1)}, u32[]{:S(2)}) copy-start(pred[384,384]{0,1:T(8,128)(4,1)} %iota_compare_fusion.1) | copy-start | bytes 442372
  226.7 13.0 %copy-start.7 = (pred[384,384]{0,1:T(8,128)(4,1)S(1)}, pred[384,384]{0,1:T(8,128)(4,1)}, u32[]{:S(2)}) copy-start(pred[384,384]{0,1:T(8,128)(4,1)} %iota_compare_fusion) | copy-start | bytes 442372
  236.7 3.0 copy-start.1
  236.7 23.7 %copy-start.6 = (pred[384,384]{0,1:T(8,128)(4,1)S(1)}, pred[384,384]{0,1:T(8,128)(4,1)}, u32[]{:S(2)}) copy-start(pred[384,384]{0,1:T(8,128)(4,1)} %iota_compare_fusion.1) | copy-start | bytes 442372
  236.7 23.7 %copy-start.8 = (pred[384,384]{0,1:T(8,128)(4,1)S(1)}, pred[384,384]{0,1:T(8,128)(4,1)}, u32[]{:S(2)}) copy-start(pred[384,384]{0,1:T(8,128)(4,1)} %iota_compare_fusion) | copy-start | bytes 442372
  260.4 13.9 %copy-start.3 = (f32[384,1024]{1,0:T(8,128)S(1)}, f32[384,1024]{1,0:T(8,128)}, u32[]{:S(2)}) copy-start(f32[384,1024]{1,0:T(8,128)} %copy-done.2) | copy-start | bytes 4718596
  273.1 1.1 copy-start.4
Sparse Core Ops, SparseCore 0:
  282.0 179.1 all-reduce.2
